TPU v7x, 32 devices: a whole 2x2x4 slice. The times are simulated.
32 devices in a mesh: group: 1, dev: 32 (over z, y, x, core).
Axes of the slice: x: 2, y: 2, z: 4, core: 2. Of those that a mesh axis runs over, the one named last changes fastest.
Arguments:
- traces: bfloat16 [2048, 1024], P(('group', 'dev')), may hold values from -6 to 6
- fetch_rows: int32 [1, 32768], P('group', 'dev'), may hold values from 0 to 2047, as said below
- pair_left: int32 [1, 1024, 32], P('group', 'dev'), may hold values from 0 to 1023
- pair_right: int32 [1, 1024, 32], P('group', 'dev'), may hold values from 0 to 1023
- taper_index: int32 [1, 1024, 32], P('group', 'dev'), may hold values from 0 to 15
- taper_table: float32 [16], replicated, may hold values from 0.1 to 1
Outputs:
- predicted: float32 [1024, 1024], P('dev', 'group')
Inputs may be any that keep to these rules, and one draw needn't show every extreme that they name: `fetch_rows`: entry j of device d's block of 1024 entries (columns d * 1024 to (d + 1) * 1024 - 1) names a trace held by device j // 32 of the group: it lies in [(j // 32) * 64, (j // 32 + 1) * 64). So every device lists exactly 32 traces of each device of its group.
All inputs are finite; a program needn't handle non-finite values.
Results may differ from a plain program's by a relative error of at most 0.0003.
Values may be sent and summed in bfloat16 or wider, within the bound.
No kernel may reach another device: no remote copies, remote signals or barrier semaphores. Data moves between devices by JAX's collectives and lax.ppermute only.
A program may use at most 64 MiB of HBM per device.

v0:
```python
import functools

import jax
import jax.numpy as jnp
from jax import lax
from jax.experimental import pallas as pl
from jax.experimental.pallas import tpu as pltpu
from jax.sharding import PartitionSpec as P


LANES = 128
ROWS = 8
PER_STEP = 8


def exchange(value, count, even, odd=None):
    odd = even if odd is None else odd
    return lax.ppermute(value, "dev", [(i, i ^ (odd if i & 1 else even)) for i in range(count)])


def gather_blocks(own, count):
    levels = {0: own}
    pieces = []

    def level_of(level):
        if level not in levels:
            low = level & -level
            levels[level] = exchange(level_of(level ^ low), count, 8 * low)
        return levels[level]

    for level in range(count // 8):
        near = exchange(level_of(level), count, 2, 4)
        both = jnp.concatenate([level_of(level), near], axis=0)
        far = exchange(both, count, 4, 2)
        pieces.append((both, 4 * level))
        pieces.append((far, 4 * level + 2))
        pieces.append((exchange(both, count, 1), count // 2 + 4 * level))
        pieces.append((exchange(far, count, 1), count // 2 + 4 * level + 2))
    return pieces


def slots_of(rows, rows_each, count):
    owner = rows // rows_each
    offset = owner ^ lax.axis_index("dev")
    plane = (offset >> 1) & 3
    swapped = ((plane & 1) << 1) | (plane >> 1)
    label = jnp.where(owner % 2 == 0, plane, swapped)
    slot = (offset & 1) * (count // 2) + (offset >> 3) * 4 + label
    return slot, rows % rows_each


def aperture_kernel(slots, rows_a, rows_b, weights, *refs, aperture, blocks, outs, scale):
    pieces = refs[: len(slots)]
    out_ref, held, left, right, sems = refs[len(slots) :]
    copies = []
    for i, (piece, slot) in enumerate(zip(pieces, slots, strict=True)):
        copies.append(pltpu.make_async_copy(piece, held.at[pl.ds(slot, piece.shape[0])], sems.at[i]))
        copies[-1].start()
    for copy in copies:
        copy.wait()
    lane = lax.broadcasted_iota(jnp.int32, (ROWS, LANES), 1)
    row = lax.broadcasted_iota(jnp.int32, (ROWS, LANES), 0)
    tile = ROWS * blocks

    def shifted(tiles, amount, carried, **how):
        rolled = [pltpu.roll(t, amount, 1, **how) for t in tiles]
        before = [jnp.zeros((ROWS, LANES), jnp.float32)] + rolled[:-1]
        return [jnp.where(carried, b, r) for b, r in zip(before, rolled, strict=True)]

    def columns(ref, p):
        return jnp.concatenate(
            [ref[pl.ds(tile * g + p, ROWS, stride=blocks), :] for g in range(aperture // ROWS)], axis=0
        )

    def one_output(o, lhs_ref, rhs_ref):
        for k in range(aperture):
            here = pl.ds(blocks * k, blocks)
            lhs_ref[here, :] = held[rows_a[o, k]].astype(jnp.float32) * weights[o, k]
            rhs_ref[here, :] = held[rows_b[o, k]].astype(jnp.float32)
        delayed = [columns(rhs_ref, p).astype(jnp.bfloat16) for p in range(blocks)]
        lhs = jnp.concatenate([columns(lhs_ref, p) for p in range(blocks)], axis=0).T
        high = lhs.astype(jnp.bfloat16)
        low = (lhs - high.astype(jnp.float32)).astype(jnp.bfloat16)
        none = jnp.zeros((aperture, LANES), jnp.bfloat16)
        products = []
        for n in range(0, blocks, 2):
            depth = aperture * (n + 2)
            rhs = jnp.concatenate(
                [
                    jnp.concatenate([delayed[n - p] if p <= n else none, delayed[n + 1 - p]], axis=1)
                    for p in range(n + 2)
                ],
                axis=0,
            )
            product = jnp.dot(high[:, :depth], rhs, preferred_element_type=jnp.float32)
            product += jnp.dot(low[:, :depth], rhs, preferred_element_type=jnp.float32)
            products += [product[:, :LANES], product[:, LANES:]]
        total = [q[LANES - ROWS :] for q in products]
        for g in range(LANES // ROWS - 2, -1, -1):
            moved = shifted(total, ROWS, lane < ROWS)
            total = [m + q[ROWS * g : ROWS * g + ROWS] for m, q in zip(moved, products, strict=True)]
        total = shifted(total, 0, lane < row, stride=1, stride_axis=0)
        sums = jnp.concatenate([jnp.sum(t, axis=0, keepdims=True) for t in total], axis=1)
        out_ref[pl.ds(o, 1), :] = sums * scale

    def step(i, carry):
        for u in range(PER_STEP):
            one_output(i * PER_STEP + u, left.at[u], right.at[u])
        return carry

    lax.fori_loop(0, outs // PER_STEP, step, 0)


def aperture_sums(rows_a, rows_b, weights, pieces, rows_each, scale):
    outs, aperture = rows_a.shape
    blocks = pieces[0][0].shape[1]
    held = sum(piece.shape[0] for piece, _ in pieces)
    work = pltpu.VMEM((PER_STEP, aperture * blocks, LANES), jnp.float32)
    return pl.pallas_call(
        functools.partial(
            aperture_kernel,
            [slot * rows_each for _, slot in pieces],
            aperture=aperture,
            blocks=blocks,
            outs=outs,
            scale=scale,
        ),
        out_shape=jax.ShapeDtypeStruct((outs, blocks * LANES), jnp.float32),
        in_specs=[pl.BlockSpec(memory_space=pltpu.SMEM)] * 3 + [pl.BlockSpec(memory_space=pl.ANY)] * len(pieces),
        out_specs=pl.BlockSpec(memory_space=pltpu.VMEM),
        scratch_shapes=[
            pltpu.VMEM((held, blocks, LANES), jnp.bfloat16),
            work,
            work,
            pltpu.SemaphoreType.DMA((len(pieces),)),
        ],
        name="aperture_sums",
    )(rows_a, rows_b, weights, *[piece for piece, _ in pieces])


def shards(traces, fetch_rows, pair_left, pair_right, taper_index, taper_table):
    rows_each, samples = traces.shape
    count = lax.axis_size("dev")
    outputs, aperture = pair_left.shape[1:]
    pieces = gather_blocks(traces.reshape(rows_each, samples // LANES, LANES), count)

    slot, row = slots_of(fetch_rows[0], rows_each, count)
    table = jnp.stack([slot, row], axis=1).astype(jnp.bfloat16)
    wanted = jnp.concatenate([pair_left[0], pair_right[0]], axis=0).reshape(-1)
    onehot = (wanted[:, None] == jnp.arange(table.shape[0], dtype=jnp.int32)[None, :]).astype(jnp.bfloat16)
    found = jnp.dot(onehot, table, preferred_element_type=jnp.float32).astype(jnp.int32)
    places = (found[:, 0] * rows_each + found[:, 1]).reshape(2, outputs, aperture)
    weights = jnp.zeros((outputs, aperture), jnp.float32)
    for j in range(taper_table.shape[0]):
        weights = jnp.where(taper_index[0] == j, taper_table[j], weights)

    scale = float(1.0 / (samples * aperture * lax.axis_size("group")) ** 0.5)
    partial = aperture_sums(places[0], places[1], weights, pieces, rows_each, scale)
    return lax.psum_scatter(partial, "group", scatter_dimension=1, tiled=True)


def solution(mesh):
    return jax.shard_map(
        shards,
        mesh=mesh,
        in_specs=(
            P(("group", "dev"), None),
            P("group", "dev"),
            P("group", "dev", None),
            P("group", "dev", None),
            P("group", "dev", None),
            P(),
        ),
        out_specs=P("dev", "group"),
        check_vma=False,
    )
```

profile of v0, /device:TPU:0, one launch (start us, length us, event | category | flops | bytes accessed | tf_op | source)
XLA Modules:
  0.0 63.7 jit_solution(15573983397514337392)
XLA Ops:
  0.0 1.0 %copy.7 = bf16[8,8,8,128]{3,2,1,0:T(8,128)(2,1)S(1)} copy(bf16[8,8,8,128]{3,1,2,0:T(8,128)(2,1)} %bitcast.42) | data formatting | bytes 262144
  1.0 4.1 %collective-permute-start.9 = (bf16[64,8,128]{2,1,0:T(8,128)(2,1)S(1)}, bf16[64,8,128]{2,1,0:T(8,128)(2,1)S(1)}, u32[]{:S(2)}, u32[]{:S(2)}) collective-permute-start(bf16[64,8,128]{2,1,0:T(8,128)(2,1)S(1)} %bitcast.38), channel_id=1, source_target_pairs={{0,16},{1,17},{2,18},{3,19},{4,20},{5,21},{6,22},{7,23},{8,24},{9,... | collective-permute-start | bytes 393224 | tf_op jit(solution)/shard_map/ppermute | solution.py:18
  5.1 1.6 %collective-permute-start.4 = (bf16[64,8,128]{2,1,0:T(8,128)(2,1)S(1)}, bf16[64,8,128]{2,1,0:T(8,128)(2,1)S(1)}, u32[]{:S(2)}, u32[]{:S(2)}) collective-permute-start(bf16[64,8,128]{2,1,0:T(8,128)(2,1)S(1)} %bitcast.39), channel_id=1, source_target_pairs={{0,8},{1,9},{2,10},{3,11},{4,12},{5,13},{6,14},{7,15},{8,0},{9,1},... | collective-permute-start | bytes 393224 | tf_op jit(solution)/shard_map/ppermute | solution.py:18
  6.7 1.5 %collective-permute-start = (bf16[64,8,128]{2,1,0:T(8,128)(2,1)S(1)}, bf16[64,8,128]{2,1,0:T(8,128)(2,1)S(1)}, u32[]{:S(2)}, u32[]{:S(2)}) collective-permute-start(bf16[64,8,128]{2,1,0:T(8,128)(2,1)S(1)} %bitcast.40), channel_id=1, source_target_pairs={{0,2},{1,5},{2,0},{3,7},{4,6},{5,1},{6,4},{7,3},{8,10},{9,13},{10,... | collective-permute-start | bytes 393224 | tf_op jit(solution)/shard_map/ppermute | solution.py:18
  8.3 0.1 eq.167
  8.4 1.8 %fusion.2 = s32[2048,2]{0,1:T(2,128)S(1)} fusion(s32[2048]{0:T(1024)S(1)} %eq.167, bf16[1024,1]{0,1:T(2,128)(2,1)S(1)} %fusion.3, bf16[1024,1]{0,1:T(2,128)(2,1)S(1)} %get-tuple-element.7), kind=kOutput, calls=%fused_computation.3 | convolution fusion | flops 10498048 | bytes 28672 | tf_op jit(solution)/shard_map/dot_general | solution.py:151
  10.2 1.4 %collective-permute-done = bf16[64,8,128]{2,1,0:T(8,128)(2,1)S(1)} collective-permute-done((bf16[64,8,128]{2,1,0:T(8,128)(2,1)S(1)}, bf16[64,8,128]{2,1,0:T(8,128)(2,1)S(1)}, u32[]{:S(2)}, u32[]{:S(2)}) %collective-permute-start) | collective-permute-done | bytes 131104 | tf_op jit(solution)/shard_map/ppermute | solution.py:18
  11.8 1.6 %collective-permute-start.1 = (bf16[128,8,128]{2,1,0:T(8,128)(2,1)S(1)}, bf16[128,8,128]{2,1,0:T(8,128)(2,1)S(1)}, u32[]{:S(2)}, u32[]{:S(2)}) collective-permute-start(bf16[128,8,128]{2,1,0:T(8,128)(2,1)S(1)} %constant_dynamic-update-slice_fusion.refs_0_), channel_id=1, source_target_pairs={{0,4},{1,3},{2,6},{3,1},{4,0},{5,7},{6,2},{7,5},{8,12},{9,11},{10,... | collective-permute-start | bytes 786440 | tf_op jit(solution)/shard_map/ppermute | solution.py:18
  13.3 0.5 collective-permute-start.14
  13.8 1.5 %collective-permute-start.10 = (bf16[64,8,128]{2,1,0:T(8,128)(2,1)S(1)}, bf16[64,8,128]{2,1,0:T(8,128)(2,1)S(1)}, u32[]{:S(2)}, u32[]{:S(2)}) collective-permute-start(bf16[64,8,128]{2,1,0:T(8,128)(2,1)S(1)} %collective-permute-done.9), channel_id=1, source_target_pairs={{0,2},{1,5},{2,0},{3,7},{4,6},{5,1},{6,4},{7,3},{8,10},{9,13},{10,... | collective-permute-start | bytes 393224 | tf_op jit(solution)/shard_map/ppermute | solution.py:18
  15.3 0.5 collective-permute-start.5
  15.9 3.2 %collective-permute-done.10 = bf16[64,8,128]{2,1,0:T(8,128)(2,1)S(1)} collective-permute-done((bf16[64,8,128]{2,1,0:T(8,128)(2,1)S(1)}, bf16[64,8,128]{2,1,0:T(8,128)(2,1)S(1)}, u32[]{:S(2)}, u32[]{:S(2)}) %collective-permute-start.10) | collective-permute-done | bytes 131104 | tf_op jit(solution)/shard_map/ppermute | solution.py:18
  19.1 0.2 collective-permute-start.12
  19.3 1.5 %collective-permute-start.15 = (bf16[64,8,128]{2,1,0:T(8,128)(2,1)S(1)}, bf16[64,8,128]{2,1,0:T(8,128)(2,1)S(1)}, u32[]{:S(2)}, u32[]{:S(2)}) collective-permute-start(bf16[64,8,128]{2,1,0:T(8,128)(2,1)S(1)} %collective-permute-done.14), channel_id=1, source_target_pairs={{0,2},{1,5},{2,0},{3,7},{4,6},{5,1},{6,4},{7,3},{8,10},{9,13},{10,... | collective-permute-start | bytes 393224 | tf_op jit(solution)/shard_map/ppermute | solution.py:18
  20.8 1.6 %collective-permute-start.11 = (bf16[128,8,128]{2,1,0:T(8,128)(2,1)S(1)}, bf16[128,8,128]{2,1,0:T(8,128)(2,1)S(1)}, u32[]{:S(2)}, u32[]{:S(2)}) collective-permute-start(bf16[128,8,128]{2,1,0:T(8,128)(2,1)S(1)} %constant_dynamic-update-slice_fusion.4.refs_8_), channel_id=1, source_target_pairs={{0,4},{1,3},{2,6},{3,1},{4,0},{5,7},{6,2},{7,5},{8,12},{9,11},{10,... | collective-permute-start | bytes 786440 | tf_op jit(solution)/shard_map/ppermute | solution.py:18
  22.4 2.4 %collective-permute-done.15 = bf16[64,8,128]{2,1,0:T(8,128)(2,1)S(1)} collective-permute-done((bf16[64,8,128]{2,1,0:T(8,128)(2,1)S(1)}, bf16[64,8,128]{2,1,0:T(8,128)(2,1)S(1)}, u32[]{:S(2)}, u32[]{:S(2)}) %collective-permute-start.15) | collective-permute-done | bytes 131104 | tf_op jit(solution)/shard_map/ppermute | solution.py:18
  24.9 1.8 %collective-permute-start.6 = (bf16[128,8,128]{2,1,0:T(8,128)(2,1)S(1)}, bf16[128,8,128]{2,1,0:T(8,128)(2,1)S(1)}, u32[]{:S(2)}, u32[]{:S(2)}) collective-permute-start(bf16[128,8,128]{2,1,0:T(8,128)(2,1)S(1)} %constant_dynamic-update-slice_fusion.2.refs_4_), channel_id=1, source_target_pairs={{0,4},{1,3},{2,6},{3,1},{4,0},{5,7},{6,2},{7,5},{8,12},{9,11},{10,... | collective-permute-start | bytes 786440 | tf_op jit(solution)/shard_map/ppermute | solution.py:18
  26.7 0.3 collective-permute-start.16
  27.1 0.1 collective-permute-done.11.refs_9_
  27.2 0.4 collective-permute-start.3
  27.6 0.1 collective-permute-start.13
  27.7 3.6 %collective-permute-done.6.refs_5_ = bf16[128,8,128]{2,1,0:T(8,128)(2,1)S(1)} collective-permute-done((bf16[128,8,128]{2,1,0:T(8,128)(2,1)S(1)}, bf16[128,8,128]{2,1,0:T(8,128)(2,1)S(1)}, u32[]{:S(2)}, u32[]{:S(2)}) %collective-permute-start.6) | collective-permute-done | bytes 262176 | tf_op jit(solution)/shard_map/ppermute | solution.py:18
  31.3 2.8 %collective-permute-done.16.refs_13_ = bf16[128,8,128]{2,1,0:T(8,128)(2,1)S(1)} collective-permute-done((bf16[128,8,128]{2,1,0:T(8,128)(2,1)S(1)}, bf16[128,8,128]{2,1,0:T(8,128)(2,1)S(1)}, u32[]{:S(2)}, u32[]{:S(2)}) %collective-permute-start.16) | collective-permute-done | bytes 262176 | tf_op jit(solution)/shard_map/ppermute | solution.py:18
  34.2 0.7 %fusion.10 = (f32[1]{0:T(128)}, f32[1]{0:T(128)}, f32[1]{0:T(128)}, f32[1]{0:T(128)}, f32[1]{0:T(128)}, /*index=5*/f32[1]{0:T(128)}, f32[1]{0:T(128)}, f32[1]{0:...) fusion(f32[16]{0:T(128)S(1)} %copy-done.15), kind=kLoop, calls=%fused_computation.37 | loop fusion | bytes 128 | tf_op jit(solution)/shard_map/slice | solution.py:155
  34.9 0.7 %slice.75.rows_b = s32[32,32]{1,0:T(8,128)} reshape(s32[1024]{0:T(1024)S(1)} %get-tuple-element.5) | data formatting | bytes 8192 | tf_op jit(solution)/shard_map/slice | solution.py:158
  35.6 0.7 %slice.73.rows_a = s32[32,32]{1,0:T(8,128)} reshape(s32[1024]{0:T(1024)S(1)} %get-tuple-element.6) | data formatting | bytes 8192 | tf_op jit(solution)/shard_map/slice | solution.py:158
  36.2 10.5 %bitcast_select_fusion.weights = f32[32,32]{1,0:T(8,128)} fusion(s32[1,32,32]{2,1,0:T(8,128)S(1)} %copy-done.16, f32[]{:T(128)} %bitcast.5, f32[]{:T(128)} %bitcast.6, f32[]{:T(128)} %bitcast.7, f32[]{:T(128)} %bitcast.8, f32[]{:T(128)} %bitcast.9, f32[]{:T(128)} %bitcast.10, f32[]{:T(128)} %bitcast.11, f32[]{:T(128)} %bitcast.12, f32[]{:T(128)} %bitcast.13, ...), kind=kLoop, calls=%fused_computation.15 | loop fusion | flops 32768 | bytes 8256 | tf_op jit(solution)/shard_map/jit(_where)/select_n | solution.py:155
  46.9 0.5 copy-done.12
  47.4 0.1 copy-done.11
  47.5 0.1 copy-done.13
  47.6 0.1 copy-done.14
  47.7 16.0 %aperture_sums.1 = f32[32,1024]{1,0:T(8,128)} custom-call(s32[32,32]{1,0:T(8,128)} %slice.73.rows_a, s32[32,32]{1,0:T(8,128)} %slice.75.rows_b, f32[32,32]{1,0:T(8,128)} %bitcast_select_fusion.weights, bf16[128,8,128]{2,1,0:T(8,128)(2,1)} %copy-done.2, bf16[128,8,128]{2,1,0:T(8,128)(2,1)} %copy-done.5, bf16[128,8,128]{2,1,0:T(8,128)(2,1)} %copy-done.4, ...), custom_call_target="tpu_custom_call" | custom-call | tf_op jit(solution)/shard_map/aperture_sums/pallas_call | solution.py:119
  (67 shorter events, 0.5 us)
Async XLA Ops:
  0.0 8.3 %copy-start.17 = (s32[1,32,32]{2,1,0:T(8,128)S(1)}, s32[1,32,32]{2,1,0:T(8,128)}, u32[]{:S(2)}) copy-start(s32[1,32,32]{2,1,0:T(8,128)} %param.9) | copy-start | bytes 12292
  0.0 8.3 %copy-start.18 = (s32[1,32,32]{2,1,0:T(8,128)S(1)}, s32[1,32,32]{2,1,0:T(8,128)}, u32[]{:S(2)}) copy-start(s32[1,32,32]{2,1,0:T(8,128)} %param.8) | copy-start | bytes 12292
  1.0 12.4 %collective-permute-start.9 = (bf16[64,8,128]{2,1,0:T(8,128)(2,1)S(1)}, bf16[64,8,128]{2,1,0:T(8,128)(2,1)S(1)}, u32[]{:S(2)}, u32[]{:S(2)}) collective-permute-start(bf16[64,8,128]{2,1,0:T(8,128)(2,1)S(1)} %bitcast.38), channel_id=1, source_target_pairs={{0,16},{1,17},{2,18},{3,19},{4,20},{5,21},{6,22},{7,23},{8,24},{9,... | collective-permute-start | bytes 393224 | tf_op jit(solution)/shard_map/ppermute | solution.py:18
  5.1 10.2 %collective-permute-start.4 = (bf16[64,8,128]{2,1,0:T(8,128)(2,1)S(1)}, bf16[64,8,128]{2,1,0:T(8,128)(2,1)S(1)}, u32[]{:S(2)}, u32[]{:S(2)}) collective-permute-start(bf16[64,8,128]{2,1,0:T(8,128)(2,1)S(1)} %bitcast.39), channel_id=1, source_target_pairs={{0,8},{1,9},{2,10},{3,11},{4,12},{5,13},{6,14},{7,15},{8,0},{9,1},... | collective-permute-start | bytes 393224 | tf_op jit(solution)/shard_map/ppermute | solution.py:18
  6.7 5.0 %collective-permute-start = (bf16[64,8,128]{2,1,0:T(8,128)(2,1)S(1)}, bf16[64,8,128]{2,1,0:T(8,128)(2,1)S(1)}, u32[]{:S(2)}, u32[]{:S(2)}) collective-permute-start(bf16[64,8,128]{2,1,0:T(8,128)(2,1)S(1)} %bitcast.40), channel_id=1, source_target_pairs={{0,2},{1,5},{2,0},{3,7},{4,6},{5,1},{6,4},{7,3},{8,10},{9,13},{10,... | collective-permute-start | bytes 393224 | tf_op jit(solution)/shard_map/ppermute | solution.py:18
  11.7 13.2 %collective-permute-start.2 = (bf16[128,8,128]{2,1,0:T(8,128)(2,1)S(1)}, bf16[128,8,128]{2,1,0:T(8,128)(2,1)S(1)}, u32[]{:S(2)}, u32[]{:S(2)}) collective-permute-start(bf16[128,8,128]{2,1,0:T(8,128)(2,1)S(1)} %constant_dynamic-update-slice_fusion.refs_0_), channel_id=1, source_target_pairs={{0,1},{1,0},{2,3},{3,2},{4,5},{5,4},{6,7},{7,6},{8,9},{9,8},{10,11... | collective-permute-start | bytes 786440 | tf_op jit(solution)/shard_map/ppermute | solution.py:18
  11.8 14.9 %collective-permute-start.1 = (bf16[128,8,128]{2,1,0:T(8,128)(2,1)S(1)}, bf16[128,8,128]{2,1,0:T(8,128)(2,1)S(1)}, u32[]{:S(2)}, u32[]{:S(2)}) collective-permute-start(bf16[128,8,128]{2,1,0:T(8,128)(2,1)S(1)} %constant_dynamic-update-slice_fusion.refs_0_), channel_id=1, source_target_pairs={{0,4},{1,3},{2,6},{3,1},{4,0},{5,7},{6,2},{7,5},{8,12},{9,11},{10,... | collective-permute-start | bytes 786440 | tf_op jit(solution)/shard_map/ppermute | solution.py:18
  13.3 5.9 %collective-permute-start.14 = (bf16[64,8,128]{2,1,0:T(8,128)(2,1)S(1)}, bf16[64,8,128]{2,1,0:T(8,128)(2,1)S(1)}, u32[]{:S(2)}, u32[]{:S(2)}) collective-permute-start(bf16[64,8,128]{2,1,0:T(8,128)(2,1)S(1)} %collective-permute-done.9), channel_id=1, source_target_pairs={{0,8},{1,9},{2,10},{3,11},{4,12},{5,13},{6,14},{7,15},{8,0},{9,1},... | collective-permute-start | bytes 393224 | tf_op jit(solution)/shard_map/ppermute | solution.py:18
  13.8 5.3 %collective-permute-start.10 = (bf16[64,8,128]{2,1,0:T(8,128)(2,1)S(1)}, bf16[64,8,128]{2,1,0:T(8,128)(2,1)S(1)}, u32[]{:S(2)}, u32[]{:S(2)}) collective-permute-start(bf16[64,8,128]{2,1,0:T(8,128)(2,1)S(1)} %collective-permute-done.9), channel_id=1, source_target_pairs={{0,2},{1,5},{2,0},{3,7},{4,6},{5,1},{6,4},{7,3},{8,10},{9,13},{10,... | collective-permute-start | bytes 393224 | tf_op jit(solution)/shard_map/ppermute | solution.py:18
  15.3 5.5 %collective-permute-start.5 = (bf16[64,8,128]{2,1,0:T(8,128)(2,1)S(1)}, bf16[64,8,128]{2,1,0:T(8,128)(2,1)S(1)}, u32[]{:S(2)}, u32[]{:S(2)}) collective-permute-start(bf16[64,8,128]{2,1,0:T(8,128)(2,1)S(1)} %collective-permute-done.4), channel_id=1, source_target_pairs={{0,2},{1,5},{2,0},{3,7},{4,6},{5,1},{6,4},{7,3},{8,10},{9,13},{10,... | collective-permute-start | bytes 393224 | tf_op jit(solution)/shard_map/ppermute | solution.py:18
  19.1 7.9 %collective-permute-start.12 = (bf16[128,8,128]{2,1,0:T(8,128)(2,1)S(1)}, bf16[128,8,128]{2,1,0:T(8,128)(2,1)S(1)}, u32[]{:S(2)}, u32[]{:S(2)}) collective-permute-start(bf16[128,8,128]{2,1,0:T(8,128)(2,1)S(1)} %constant_dynamic-update-slice_fusion.4.refs_8_), channel_id=1, source_target_pairs={{0,1},{1,0},{2,3},{3,2},{4,5},{5,4},{6,7},{7,6},{8,9},{9,8},{10,11... | collective-permute-start | bytes 786440 | tf_op jit(solution)/shard_map/ppermute | solution.py:18
  19.3 5.6 %collective-permute-start.15 = (bf16[64,8,128]{2,1,0:T(8,128)(2,1)S(1)}, bf16[64,8,128]{2,1,0:T(8,128)(2,1)S(1)}, u32[]{:S(2)}, u32[]{:S(2)}) collective-permute-start(bf16[64,8,128]{2,1,0:T(8,128)(2,1)S(1)} %collective-permute-done.14), channel_id=1, source_target_pairs={{0,2},{1,5},{2,0},{3,7},{4,6},{5,1},{6,4},{7,3},{8,10},{9,13},{10,... | collective-permute-start | bytes 393224 | tf_op jit(solution)/shard_map/ppermute | solution.py:18
  20.8 13.4 %copy-start.15 = (f32[16]{0:T(128)S(1)}, f32[16]{0:T(128)}, u32[]{:S(2)}) copy-start(f32[16]{0:T(128)} %param.11) | copy-start | bytes 196
  20.8 6.4 %collective-permute-start.11 = (bf16[128,8,128]{2,1,0:T(8,128)(2,1)S(1)}, bf16[128,8,128]{2,1,0:T(8,128)(2,1)S(1)}, u32[]{:S(2)}, u32[]{:S(2)}) collective-permute-start(bf16[128,8,128]{2,1,0:T(8,128)(2,1)S(1)} %constant_dynamic-update-slice_fusion.4.refs_8_), channel_id=1, source_target_pairs={{0,4},{1,3},{2,6},{3,1},{4,0},{5,7},{6,2},{7,5},{8,12},{9,11},{10,... | collective-permute-start | bytes 786440 | tf_op jit(solution)/shard_map/ppermute | solution.py:18
  22.4 24.4 %copy-start = (bf16[128,8,128]{2,1,0:T(8,128)(2,1)}, bf16[128,8,128]{2,1,0:T(8,128)(2,1)S(1)}, u32[]{:S(2)}) copy-start(bf16[128,8,128]{2,1,0:T(8,128)(2,1)S(1)} %constant_dynamic-update-slice_fusion.2.refs_4_) | copy-start | bytes 786436
  22.4 13.8 %copy-start.16 = (s32[1,32,32]{2,1,0:T(8,128)S(1)}, s32[1,32,32]{2,1,0:T(8,128)}, u32[]{:S(2)}) copy-start(s32[1,32,32]{2,1,0:T(8,128)} %param.10) | copy-start | bytes 12292
  24.8 2.8 %collective-permute-start.7 = (bf16[128,8,128]{2,1,0:T(8,128)(2,1)S(1)}, bf16[128,8,128]{2,1,0:T(8,128)(2,1)S(1)}, u32[]{:S(2)}, u32[]{:S(2)}) collective-permute-start(bf16[128,8,128]{2,1,0:T(8,128)(2,1)S(1)} %constant_dynamic-update-slice_fusion.2.refs_4_), channel_id=1, source_target_pairs={{0,1},{1,0},{2,3},{3,2},{4,5},{5,4},{6,7},{7,6},{8,9},{9,8},{10,11... | collective-permute-start | bytes 786440 | tf_op jit(solution)/shard_map/ppermute | solution.py:18
  24.9 21.9 %copy-start.1 = (bf16[128,8,128]{2,1,0:T(8,128)(2,1)}, bf16[128,8,128]{2,1,0:T(8,128)(2,1)S(1)}, u32[]{:S(2)}) copy-start(bf16[128,8,128]{2,1,0:T(8,128)(2,1)S(1)} %constant_dynamic-update-slice_fusion.6.refs_12_) | copy-start | bytes 786436
  24.9 21.9 %copy-start.4 = (bf16[128,8,128]{2,1,0:T(8,128)(2,1)}, bf16[128,8,128]{2,1,0:T(8,128)(2,1)S(1)}, u32[]{:S(2)}) copy-start(bf16[128,8,128]{2,1,0:T(8,128)(2,1)S(1)} %collective-permute-done.2.refs_2_) | copy-start | bytes 786436
  24.9 6.4 %collective-permute-start.6 = (bf16[128,8,128]{2,1,0:T(8,128)(2,1)S(1)}, bf16[128,8,128]{2,1,0:T(8,128)(2,1)S(1)}, u32[]{:S(2)}, u32[]{:S(2)}) collective-permute-start(bf16[128,8,128]{2,1,0:T(8,128)(2,1)S(1)} %constant_dynamic-update-slice_fusion.2.refs_4_), channel_id=1, source_target_pairs={{0,4},{1,3},{2,6},{3,1},{4,0},{5,7},{6,2},{7,5},{8,12},{9,11},{10,... | collective-permute-start | bytes 786440 | tf_op jit(solution)/shard_map/ppermute | solution.py:18
  26.7 20.2 %copy-start.5 = (bf16[128,8,128]{2,1,0:T(8,128)(2,1)}, bf16[128,8,128]{2,1,0:T(8,128)(2,1)S(1)}, u32[]{:S(2)}) copy-start(bf16[128,8,128]{2,1,0:T(8,128)(2,1)S(1)} %collective-permute-done.1.refs_1_) | copy-start | bytes 786436
  26.7 7.5 %collective-permute-start.16 = (bf16[128,8,128]{2,1,0:T(8,128)(2,1)S(1)}, bf16[128,8,128]{2,1,0:T(8,128)(2,1)S(1)}, u32[]{:S(2)}, u32[]{:S(2)}) collective-permute-start(bf16[128,8,128]{2,1,0:T(8,128)(2,1)S(1)} %constant_dynamic-update-slice_fusion.6.refs_12_), channel_id=1, source_target_pairs={{0,4},{1,3},{2,6},{3,1},{4,0},{5,7},{6,2},{7,5},{8,12},{9,11},{10,... | collective-permute-start | bytes 786440 | tf_op jit(solution)/shard_map/ppermute | solution.py:18
  27.1 19.8 %copy-start.6 = (bf16[128,8,128]{2,1,0:T(8,128)(2,1)}, bf16[128,8,128]{2,1,0:T(8,128)(2,1)S(1)}, u32[]{:S(2)}) copy-start(bf16[128,8,128]{2,1,0:T(8,128)(2,1)S(1)} %collective-permute-done.12.refs_10_) | copy-start | bytes 786436
  27.1 19.7 %collective-permute-start.17 = (bf16[128,8,128]{2,1,0:T(8,128)(2,1)S(1)}, bf16[128,8,128]{2,1,0:T(8,128)(2,1)S(1)}, u32[]{:S(2)}, u32[]{:S(2)}) collective-permute-start(bf16[128,8,128]{2,1,0:T(8,128)(2,1)S(1)} %constant_dynamic-update-slice_fusion.6.refs_12_), channel_id=1, source_target_pairs={{0,1},{1,0},{2,3},{3,2},{4,5},{5,4},{6,7},{7,6},{8,9},{9,8},{10,11... | collective-permute-start | bytes 786440 | tf_op jit(solution)/shard_map/ppermute | solution.py:18
  27.2 19.6 %copy-start.7 = (bf16[128,8,128]{2,1,0:T(8,128)(2,1)}, bf16[128,8,128]{2,1,0:T(8,128)(2,1)S(1)}, u32[]{:S(2)}) copy-start(bf16[128,8,128]{2,1,0:T(8,128)(2,1)S(1)} %collective-permute-done.11.refs_9_) | copy-start | bytes 786436
  27.2 19.5 %collective-permute-start.3 = (bf16[128,8,128]{2,1,0:T(8,128)(2,1)S(1)}, bf16[128,8,128]{2,1,0:T(8,128)(2,1)S(1)}, u32[]{:S(2)}, u32[]{:S(2)}) collective-permute-start(bf16[128,8,128]{2,1,0:T(8,128)(2,1)S(1)} %collective-permute-done.1.refs_1_), channel_id=1, source_target_pairs={{0,1},{1,0},{2,3},{3,2},{4,5},{5,4},{6,7},{7,6},{8,9},{9,8},{10,11... | collective-permute-start | bytes 786440 | tf_op jit(solution)/shard_map/ppermute | solution.py:18
  27.6 19.2 %copy-start.8 = (bf16[128,8,128]{2,1,0:T(8,128)(2,1)}, bf16[128,8,128]{2,1,0:T(8,128)(2,1)S(1)}, u32[]{:S(2)}) copy-start(bf16[128,8,128]{2,1,0:T(8,128)(2,1)S(1)} %collective-permute-done.7.refs_6_) | copy-start | bytes 786436
  27.6 19.1 %collective-permute-start.13 = (bf16[128,8,128]{2,1,0:T(8,128)(2,1)S(1)}, bf16[128,8,128]{2,1,0:T(8,128)(2,1)S(1)}, u32[]{:S(2)}, u32[]{:S(2)}) collective-permute-start(bf16[128,8,128]{2,1,0:T(8,128)(2,1)S(1)} %collective-permute-done.11.refs_9_), channel_id=1, source_target_pairs={{0,1},{1,0},{2,3},{3,2},{4,5},{5,4},{6,7},{7,6},{8,9},{9,8},{10,11... | collective-permute-start | bytes 786440 | tf_op jit(solution)/shard_map/ppermute | solution.py:18
  31.3 15.5 %copy-start.9 = (bf16[128,8,128]{2,1,0:T(8,128)(2,1)}, bf16[128,8,128]{2,1,0:T(8,128)(2,1)S(1)}, u32[]{:S(2)}) copy-start(bf16[128,8,128]{2,1,0:T(8,128)(2,1)S(1)} %collective-permute-done.6.refs_5_) | copy-start | bytes 786436
  31.3 15.4 %collective-permute-start.8 = (bf16[128,8,128]{2,1,0:T(8,128)(2,1)S(1)}, bf16[128,8,128]{2,1,0:T(8,128)(2,1)S(1)}, u32[]{:S(2)}, u32[]{:S(2)}) collective-permute-start(bf16[128,8,128]{2,1,0:T(8,128)(2,1)S(1)} %collective-permute-done.6.refs_5_), channel_id=1, source_target_pairs={{0,1},{1,0},{2,3},{3,2},{4,5},{5,4},{6,7},{7,6},{8,9},{9,8},{10,11... | collective-permute-start | bytes 786440 | tf_op jit(solution)/shard_map/ppermute | solution.py:18
  34.1 12.7 %copy-start.10 = (bf16[128,8,128]{2,1,0:T(8,128)(2,1)}, bf16[128,8,128]{2,1,0:T(8,128)(2,1)S(1)}, u32[]{:S(2)}) copy-start(bf16[128,8,128]{2,1,0:T(8,128)(2,1)S(1)} %collective-permute-done.16.refs_13_) | copy-start | bytes 786436
  34.1 12.6 %collective-permute-start.18 = (bf16[128,8,128]{2,1,0:T(8,128)(2,1)S(1)}, bf16[128,8,128]{2,1,0:T(8,128)(2,1)}, u32[]{:S(2)}, u32[]{:S(2)}) collective-permute-start(bf16[128,8,128]{2,1,0:T(8,128)(2,1)S(1)} %collective-permute-done.16.refs_13_), channel_id=1, source_target_pairs={{0,1},{1,0},{2,3},{3,2},{4,5},{5,4},{6,7},{7,6},{8,9},{9,8},{10,11... | collective-permute-start | bytes 786440 | tf_op jit(solution)/shard_map/ppermute | solution.py:18
  (7 other events, 19.0 us)
where the time goes:
time: 64.1 us; the launch traced here: 63.7 us
  starting transfers between devices  17.3 us (27%)
  Pallas kernels  16 us (25%)
  waiting for transfers between devices  13.5 us (21%)
  other arithmetic  10.6 us (17%)
  local copies, waits for them, and re-layouts  4.11 us (6%)
  matrix products  1.85 us (3%)
    ppermute x19, starting transfers between devices, exchange(): lax.ppermute(value, 'dev', [(i, i ^ (odd if i & 1 else even)) for i in ra...  17.3 us
    pallas_call x1, Pallas kernels, aperture_sums(): pl.pallas_call(functools.partial(aperture_kernel, [slot * rows_each for _...  16 us
    ppermute x19, waiting for transfers between devices, exchange(): lax.ppermute(value, 'dev', [(i, i ^ (odd if i & 1 else even)) for i in ra...  13.5 us
    select_n x1, other arithmetic, shards(): weights = jnp.where(taper_index[0] == j, taper_table[j], weights)  10.5 us
    unnamed x45, local copies, waits for them, and re-layouts  1.88 us
    dot_general x1, matrix products, shards(): jnp.dot(onehot, table, preferred_element_type=jnp.float32).astype(jnp.int32)  1.85 us
  transfers between devices with their start and end apart: 19, of which 6 were waited for; matrix products, arithmetic and copies ran while one was open for 23% of the time, Pallas kernels for 0%

commit v1 on v0

--- a/solution.py
+++ b/solution.py
@@ -49,7 +49,7 @@
     return slot, rows % rows_each
 
 
-def aperture_kernel(slots, rows_a, rows_b, weights, *refs, aperture, blocks, outs, scale):
+def aperture_kernel(slots, places, tapers, table, *refs, aperture, blocks, outs, scale):
     pieces = refs[: len(slots)]
     out_ref, held, left, right, sems = refs[len(slots) :]
     copies = []
@@ -75,8 +75,9 @@
     def one_output(o, lhs_ref, rhs_ref):
         for k in range(aperture):
             here = pl.ds(blocks * k, blocks)
-            lhs_ref[here, :] = held[rows_a[o, k]].astype(jnp.float32) * weights[o, k]
-            rhs_ref[here, :] = held[rows_b[o, k]].astype(jnp.float32)
+            pair = o * aperture + k
+            lhs_ref[here, :] = held[places[0, pair]].astype(jnp.float32) * table[tapers[o, k]]
+            rhs_ref[here, :] = held[places[0, outs * aperture + pair]].astype(jnp.float32)
         delayed = [columns(rhs_ref, p).astype(jnp.bfloat16) for p in range(blocks)]
         lhs = jnp.concatenate([columns(lhs_ref, p) for p in range(blocks)], axis=0).T
         high = lhs.astype(jnp.bfloat16)
@@ -111,8 +112,8 @@
     lax.fori_loop(0, outs // PER_STEP, step, 0)
 
 
-def aperture_sums(rows_a, rows_b, weights, pieces, rows_each, scale):
-    outs, aperture = rows_a.shape
+def aperture_sums(places, tapers, table, pieces, rows_each, scale):
+    outs, aperture = tapers.shape
     blocks = pieces[0][0].shape[1]
     held = sum(piece.shape[0] for piece, _ in pieces)
     work = pltpu.VMEM((PER_STEP, aperture * blocks, LANES), jnp.float32)
@@ -135,27 +136,24 @@
             pltpu.SemaphoreType.DMA((len(pieces),)),
         ],
         name="aperture_sums",
-    )(rows_a, rows_b, weights, *[piece for piece, _ in pieces])
+    )(places, tapers, table, *[piece for piece, _ in pieces])
 
 
 def shards(traces, fetch_rows, pair_left, pair_right, taper_index, taper_table):
     rows_each, samples = traces.shape
     count = lax.axis_size("dev")
-    outputs, aperture = pair_left.shape[1:]
+    _, aperture = pair_left.shape[1:]
     pieces = gather_blocks(traces.reshape(rows_each, samples // LANES, LANES), count)
 
-    slot, row = slots_of(fetch_rows[0], rows_each, count)
-    table = jnp.stack([slot, row], axis=1).astype(jnp.bfloat16)
-    wanted = jnp.concatenate([pair_left[0], pair_right[0]], axis=0).reshape(-1)
-    onehot = (wanted[:, None] == jnp.arange(table.shape[0], dtype=jnp.int32)[None, :]).astype(jnp.bfloat16)
-    found = jnp.dot(onehot, table, preferred_element_type=jnp.float32).astype(jnp.int32)
-    places = (found[:, 0] * rows_each + found[:, 1]).reshape(2, outputs, aperture)
-    weights = jnp.zeros((outputs, aperture), jnp.float32)
-    for j in range(taper_table.shape[0]):
-        weights = jnp.where(taper_index[0] == j, taper_table[j], weights)
+    slot, row = slots_of(fetch_rows, rows_each, count)
+    digits = jnp.concatenate([slot, row], axis=0).astype(jnp.bfloat16)
+    wanted = jnp.concatenate([pair_left.reshape(1, -1), pair_right.reshape(1, -1)], axis=1)
+    listed = lax.broadcasted_iota(jnp.int32, (digits.shape[1], wanted.shape[1]), 0)
+    found = jnp.dot(digits, (listed == wanted).astype(jnp.bfloat16), preferred_element_type=jnp.float32)
+    places = (found[:1] * rows_each + found[1:]).astype(jnp.int32)
 
     scale = float(1.0 / (samples * aperture * lax.axis_size("group")) ** 0.5)
-    partial = aperture_sums(places[0], places[1], weights, pieces, rows_each, scale)
+    partial = aperture_sums(places, taper_index[0], taper_table, pieces, rows_each, scale)
     return lax.psum_scatter(partial, "group", scatter_dimension=1, tiled=True)
 
 

time: 64.1 us -> 52.2 us (0.81)
  other arithmetic: 10.6 us -> 0.74 us
  local copies, waits for them, and re-layouts: 4.11 us -> 1.95 us
  waiting for transfers between devices: 13.5 us -> 14.5 us
    select_n x1 -> x0, other arithmetic: 10.5 us -> none  [shards(): weights = jnp.where(taper_index[0] == j, taper_table[j], weights)]
    slice x4 -> x0, local copies, waits for them, and re-layouts: 2.08 us -> none  [the longest x1 0.72 us: shards(): weights = jnp.where(taper_index[0] == j, taper_table[j], weights)]
    ppermute x19, waiting for transfers between devices: 13.5 us -> 14.5 us  [exchange(): lax.ppermute(value, 'dev', [(i, i ^ (odd if i & 1 else even)) for i in ra...]
    convert_element_type x0 -> x1, other arithmetic: none -> 0.67 us  [shards(): places = (found[:1] * rows_each + found[1:]).astype(jnp.int32)]
    unnamed x45 -> x43, local copies, waits for them, and re-layouts: 1.88 us -> 1.72 us
  transfers between devices with their start and end apart: 19 -> 19, of which waited for: 6 -> 6; matrix products, arithmetic and copies ran while one was open for 23% -> 5% of each run, Pallas kernels for 0% -> 0%
where the time goes in v1:
time: 52.2 us; the launch traced here: 52 us
  starting transfers between devices  17.4 us (33%)
  Pallas kernels  15.6 us (30%)
  waiting for transfers between devices  14.5 us (28%)
  local copies, waits for them, and re-layouts  1.95 us (4%)
  matrix products  1.52 us (3%)
  other arithmetic  0.74 us (1%)
    ppermute x19, starting transfers between devices, exchange(): lax.ppermute(value, 'dev', [(i, i ^ (odd if i & 1 else even)) for i in ra...  17.4 us
    pallas_call x1, Pallas kernels, aperture_sums(): pl.pallas_call(functools.partial(aperture_kernel, [slot * rows_each for _...  15.6 us
    ppermute x19, waiting for transfers between devices, exchange(): lax.ppermute(value, 'dev', [(i, i ^ (odd if i & 1 else even)) for i in ra...  14.5 us
    unnamed x43, local copies, waits for them, and re-layouts  1.72 us
    dot_general x1, matrix products, shards(): jnp.dot(digits, (listed == wanted).astype(jnp.bfloat16), preferred_elemen...  1.52 us
  transfers between devices with their start and end apart: 19, of which 6 were waited for; matrix products, arithmetic and copies ran while one was open for 5% of the time, Pallas kernels for 0%

profile of v1, /device:TPU:0, one launch (start us, length us, event | category | flops | bytes accessed | tf_op | source)
XLA Modules:
  0.0 52.0 jit_solution(12716788531164490225)
XLA Ops:
  0.0 1.0 %copy.7 = bf16[8,8,8,128]{3,2,1,0:T(8,128)(2,1)S(1)} copy(bf16[8,8,8,128]{3,1,2,0:T(8,128)(2,1)} %bitcast.8) | data formatting | bytes 262144
  1.0 4.1 %collective-permute-start.9 = (bf16[64,8,128]{2,1,0:T(8,128)(2,1)S(1)}, bf16[64,8,128]{2,1,0:T(8,128)(2,1)S(1)}, u32[]{:S(2)}, u32[]{:S(2)}) collective-permute-start(bf16[64,8,128]{2,1,0:T(8,128)(2,1)S(1)} %bitcast.4), channel_id=1, source_target_pairs={{0,16},{1,17},{2,18},{3,19},{4,20},{5,21},{6,22},{7,23},{8,24},{9,... | collective-permute-start | bytes 393224 | tf_op jit(solution)/shard_map/ppermute | solution.py:18
  5.1 1.6 %collective-permute-start.4 = (bf16[64,8,128]{2,1,0:T(8,128)(2,1)S(1)}, bf16[64,8,128]{2,1,0:T(8,128)(2,1)S(1)}, u32[]{:S(2)}, u32[]{:S(2)}) collective-permute-start(bf16[64,8,128]{2,1,0:T(8,128)(2,1)S(1)} %bitcast.5), channel_id=1, source_target_pairs={{0,8},{1,9},{2,10},{3,11},{4,12},{5,13},{6,14},{7,15},{8,0},{9,1},... | collective-permute-start | bytes 393224 | tf_op jit(solution)/shard_map/ppermute | solution.py:18
  6.7 1.5 %collective-permute-start = (bf16[64,8,128]{2,1,0:T(8,128)(2,1)S(1)}, bf16[64,8,128]{2,1,0:T(8,128)(2,1)S(1)}, u32[]{:S(2)}, u32[]{:S(2)}) collective-permute-start(bf16[64,8,128]{2,1,0:T(8,128)(2,1)S(1)} %bitcast.6), channel_id=1, source_target_pairs={{0,2},{1,5},{2,0},{3,7},{4,6},{5,1},{6,4},{7,3},{8,10},{9,13},{10,... | collective-permute-start | bytes 393224 | tf_op jit(solution)/shard_map/ppermute | solution.py:18
  8.2 0.1 add_convert_fusion
  8.3 0.1 reshape.9
  8.4 0.1 reshape.10
  8.4 3.2 %collective-permute-done = bf16[64,8,128]{2,1,0:T(8,128)(2,1)S(1)} collective-permute-done((bf16[64,8,128]{2,1,0:T(8,128)(2,1)S(1)}, bf16[64,8,128]{2,1,0:T(8,128)(2,1)S(1)}, u32[]{:S(2)}, u32[]{:S(2)}) %collective-permute-start) | collective-permute-done | bytes 131104 | tf_op jit(solution)/shard_map/ppermute | solution.py:18
  11.7 0.1 collective-permute-start.2
  11.8 1.6 %collective-permute-start.1 = (bf16[128,8,128]{2,1,0:T(8,128)(2,1)S(1)}, bf16[128,8,128]{2,1,0:T(8,128)(2,1)S(1)}, u32[]{:S(2)}, u32[]{:S(2)}) collective-permute-start(bf16[128,8,128]{2,1,0:T(8,128)(2,1)S(1)} %constant_dynamic-update-slice_fusion.refs_0_), channel_id=1, source_target_pairs={{0,4},{1,3},{2,6},{3,1},{4,0},{5,7},{6,2},{7,5},{8,12},{9,11},{10,... | collective-permute-start | bytes 786440 | tf_op jit(solution)/shard_map/ppermute | solution.py:18
  13.3 0.0 collective-permute-done.9
  13.3 0.5 collective-permute-start.14
  13.8 1.5 %collective-permute-start.10 = (bf16[64,8,128]{2,1,0:T(8,128)(2,1)S(1)}, bf16[64,8,128]{2,1,0:T(8,128)(2,1)S(1)}, u32[]{:S(2)}, u32[]{:S(2)}) collective-permute-start(bf16[64,8,128]{2,1,0:T(8,128)(2,1)S(1)} %collective-permute-done.9), channel_id=1, source_target_pairs={{0,2},{1,5},{2,0},{3,7},{4,6},{5,1},{6,4},{7,3},{8,10},{9,13},{10,... | collective-permute-start | bytes 393224 | tf_op jit(solution)/shard_map/ppermute | solution.py:18
  15.3 0.5 %collective-permute-start.5 = (bf16[64,8,128]{2,1,0:T(8,128)(2,1)S(1)}, bf16[64,8,128]{2,1,0:T(8,128)(2,1)S(1)}, u32[]{:S(2)}, u32[]{:S(2)}) collective-permute-start(bf16[64,8,128]{2,1,0:T(8,128)(2,1)S(1)} %collective-permute-done.4), channel_id=1, source_target_pairs={{0,2},{1,5},{2,0},{3,7},{4,6},{5,1},{6,4},{7,3},{8,10},{9,13},{10,... | collective-permute-start | bytes 393224 | tf_op jit(solution)/shard_map/ppermute | solution.py:18
  15.9 3.2 %collective-permute-done.10 = bf16[64,8,128]{2,1,0:T(8,128)(2,1)S(1)} collective-permute-done((bf16[64,8,128]{2,1,0:T(8,128)(2,1)S(1)}, bf16[64,8,128]{2,1,0:T(8,128)(2,1)S(1)}, u32[]{:S(2)}, u32[]{:S(2)}) %collective-permute-start.10) | collective-permute-done | bytes 131104 | tf_op jit(solution)/shard_map/ppermute | solution.py:18
  19.1 0.2 collective-permute-start.12
  19.3 1.5 %collective-permute-start.15 = (bf16[64,8,128]{2,1,0:T(8,128)(2,1)S(1)}, bf16[64,8,128]{2,1,0:T(8,128)(2,1)S(1)}, u32[]{:S(2)}, u32[]{:S(2)}) collective-permute-start(bf16[64,8,128]{2,1,0:T(8,128)(2,1)S(1)} %collective-permute-done.14), channel_id=1, source_target_pairs={{0,2},{1,5},{2,0},{3,7},{4,6},{5,1},{6,4},{7,3},{8,10},{9,13},{10,... | collective-permute-start | bytes 393224 | tf_op jit(solution)/shard_map/ppermute | solution.py:18
  20.8 1.6 %collective-permute-start.11 = (bf16[128,8,128]{2,1,0:T(8,128)(2,1)S(1)}, bf16[128,8,128]{2,1,0:T(8,128)(2,1)S(1)}, u32[]{:S(2)}, u32[]{:S(2)}) collective-permute-start(bf16[128,8,128]{2,1,0:T(8,128)(2,1)S(1)} %constant_dynamic-update-slice_fusion.4.refs_8_), channel_id=1, source_target_pairs={{0,4},{1,3},{2,6},{3,1},{4,0},{5,7},{6,2},{7,5},{8,12},{9,11},{10,... | collective-permute-start | bytes 786440 | tf_op jit(solution)/shard_map/ppermute | solution.py:18
  22.4 2.5 %collective-permute-done.15 = bf16[64,8,128]{2,1,0:T(8,128)(2,1)S(1)} collective-permute-done((bf16[64,8,128]{2,1,0:T(8,128)(2,1)S(1)}, bf16[64,8,128]{2,1,0:T(8,128)(2,1)S(1)}, u32[]{:S(2)}, u32[]{:S(2)}) %collective-permute-start.15) | collective-permute-done | bytes 131104 | tf_op jit(solution)/shard_map/ppermute | solution.py:18
  24.9 1.8 %collective-permute-start.6 = (bf16[128,8,128]{2,1,0:T(8,128)(2,1)S(1)}, bf16[128,8,128]{2,1,0:T(8,128)(2,1)S(1)}, u32[]{:S(2)}, u32[]{:S(2)}) collective-permute-start(bf16[128,8,128]{2,1,0:T(8,128)(2,1)S(1)} %constant_dynamic-update-slice_fusion.2.refs_4_), channel_id=1, source_target_pairs={{0,4},{1,3},{2,6},{3,1},{4,0},{5,7},{6,2},{7,5},{8,12},{9,11},{10,... | collective-permute-start | bytes 786440 | tf_op jit(solution)/shard_map/ppermute | solution.py:18
  26.7 0.3 collective-permute-start.16
  27.0 1.5 %fusion = f32[2,2048]{1,0:T(2,128)S(1)} fusion(s32[2048]{0:T(1024)S(1)} %bitcast.10, bf16[1,1024]{1,0:T(2,128)(2,1)S(1)} %fusion.3, bf16[1,1024]{1,0:T(2,128)(2,1)S(1)} %get-tuple-element.5), kind=kOutput, calls=%fused_computation.1 | convolution fusion | flops 10493952 | bytes 28672 | tf_op jit(solution)/shard_map/dot_general | solution.py:152
  28.6 0.1 collective-permute-start.17
  28.7 0.5 %collective-permute-start.3 = (bf16[128,8,128]{2,1,0:T(8,128)(2,1)S(1)}, bf16[128,8,128]{2,1,0:T(8,128)(2,1)S(1)}, u32[]{:S(2)}, u32[]{:S(2)}) collective-permute-start(bf16[128,8,128]{2,1,0:T(8,128)(2,1)S(1)} %collective-permute-done.1.refs_1_), channel_id=1, source_target_pairs={{0,1},{1,0},{2,3},{3,2},{4,5},{5,4},{6,7},{7,6},{8,9},{9,8},{10,11... | collective-permute-start | bytes 786440 | tf_op jit(solution)/shard_map/ppermute | solution.py:18
  29.2 0.1 collective-permute-start.13
  29.3 2.0 %collective-permute-done.6.refs_5_ = bf16[128,8,128]{2,1,0:T(8,128)(2,1)S(1)} collective-permute-done((bf16[128,8,128]{2,1,0:T(8,128)(2,1)S(1)}, bf16[128,8,128]{2,1,0:T(8,128)(2,1)S(1)}, u32[]{:S(2)}, u32[]{:S(2)}) %collective-permute-start.6) | collective-permute-done | bytes 262176 | tf_op jit(solution)/shard_map/ppermute | solution.py:18
  31.4 2.8 %collective-permute-done.16.refs_13_ = bf16[128,8,128]{2,1,0:T(8,128)(2,1)S(1)} collective-permute-done((bf16[128,8,128]{2,1,0:T(8,128)(2,1)S(1)}, bf16[128,8,128]{2,1,0:T(8,128)(2,1)S(1)}, u32[]{:S(2)}, u32[]{:S(2)}) %collective-permute-start.16) | collective-permute-done | bytes 262176 | tf_op jit(solution)/shard_map/ppermute | solution.py:18
  34.2 0.7 %fusion.2.places = s32[1,2048]{1,0:T(1,128)} fusion(f32[2,2048]{1,0:T(2,128)S(1)} %fusion), kind=kLoop, calls=%fused_computation.21 | loop fusion | flops 6144 | bytes 24576 | tf_op jit(solution)/shard_map/convert_element_type | solution.py:153
  34.9 0.8 %collective-permute-done.18.refs_15_ = bf16[128,8,128]{2,1,0:T(8,128)(2,1)S(1)} collective-permute-done((bf16[128,8,128]{2,1,0:T(8,128)(2,1)S(1)}, bf16[128,8,128]{2,1,0:T(8,128)(2,1)S(1)}, u32[]{:S(2)}, u32[]{:S(2)}) %collective-permute-start.18) | collective-permute-done | bytes 262176 | tf_op jit(solution)/shard_map/ppermute | solution.py:18
  35.8 0.1 copy-done.14
  35.8 0.6 %copy-done.15 = bf16[128,8,128]{2,1,0:T(8,128)(2,1)} copy-done((bf16[128,8,128]{2,1,0:T(8,128)(2,1)}, bf16[128,8,128]{2,1,0:T(8,128)(2,1)S(1)}, u32[]{:S(2)}) %copy-start.15) | copy-done | bytes 262168
  36.4 15.6 %aperture_sums.1 = f32[32,1024]{1,0:T(8,128)} custom-call(s32[1,2048]{1,0:T(1,128)} %fusion.2.places, s32[32,32]{1,0:T(8,128)} %bitcast.9, f32[16]{0:T(128)} %table.1, bf16[128,8,128]{2,1,0:T(8,128)(2,1)} %copy-done.2, bf16[128,8,128]{2,1,0:T(8,128)(2,1)} %copy-done.5, bf16[128,8,128]{2,1,0:T(8,128)(2,1)} %copy-done.4, bf16[128,8,128]{2,1,0:T(8,128)(2,1)} %copy-done.12, ...), custom_call_target="tpu_custom_call" | custom-call | tf_op jit(solution)/shard_map/aperture_sums/pallas_call | solution.py:120
  (61 shorter events, 0.2 us)
Async XLA Ops:
  0.0 8.2 %copy-start.18 = (s32[1,1024]{1,0:T(1,128)S(1)}, s32[1,1024]{1,0:T(1,128)}, u32[]{:S(2)}) copy-start(s32[1,1024]{1,0:T(1,128)} %param.7) | copy-start | bytes 12292
  0.0 8.3 %copy-start.16 = (s32[1,32,32]{2,1,0:T(8,128)S(1)}, s32[1,32,32]{2,1,0:T(8,128)}, u32[]{:S(2)}) copy-start(s32[1,32,32]{2,1,0:T(8,128)} %param.8) | copy-start | bytes 12292
  0.0 8.4 %copy-start.17 = (s32[1,32,32]{2,1,0:T(8,128)S(1)}, s32[1,32,32]{2,1,0:T(8,128)}, u32[]{:S(2)}) copy-start(s32[1,32,32]{2,1,0:T(8,128)} %param.9) | copy-start | bytes 12292
  1.0 12.4 %collective-permute-start.9 = (bf16[64,8,128]{2,1,0:T(8,128)(2,1)S(1)}, bf16[64,8,128]{2,1,0:T(8,128)(2,1)S(1)}, u32[]{:S(2)}, u32[]{:S(2)}) collective-permute-start(bf16[64,8,128]{2,1,0:T(8,128)(2,1)S(1)} %bitcast.4), channel_id=1, source_target_pairs={{0,16},{1,17},{2,18},{3,19},{4,20},{5,21},{6,22},{7,23},{8,24},{9,... | collective-permute-start | bytes 393224 | tf_op jit(solution)/shard_map/ppermute | solution.py:18
  5.1 10.2 %collective-permute-start.4 = (bf16[64,8,128]{2,1,0:T(8,128)(2,1)S(1)}, bf16[64,8,128]{2,1,0:T(8,128)(2,1)S(1)}, u32[]{:S(2)}, u32[]{:S(2)}) collective-permute-start(bf16[64,8,128]{2,1,0:T(8,128)(2,1)S(1)} %bitcast.5), channel_id=1, source_target_pairs={{0,8},{1,9},{2,10},{3,11},{4,12},{5,13},{6,14},{7,15},{8,0},{9,1},... | collective-permute-start | bytes 393224 | tf_op jit(solution)/shard_map/ppermute | solution.py:18
  6.7 5.0 %collective-permute-start = (bf16[64,8,128]{2,1,0:T(8,128)(2,1)S(1)}, bf16[64,8,128]{2,1,0:T(8,128)(2,1)S(1)}, u32[]{:S(2)}, u32[]{:S(2)}) collective-permute-start(bf16[64,8,128]{2,1,0:T(8,128)(2,1)S(1)} %bitcast.6), channel_id=1, source_target_pairs={{0,2},{1,5},{2,0},{3,7},{4,6},{5,1},{6,4},{7,3},{8,10},{9,13},{10,... | collective-permute-start | bytes 393224 | tf_op jit(solution)/shard_map/ppermute | solution.py:18
  11.7 7.4 %copy-start.2 = (bf16[128,8,128]{2,1,0:T(8,128)(2,1)}, bf16[128,8,128]{2,1,0:T(8,128)(2,1)S(1)}, u32[]{:S(2)}) copy-start(bf16[128,8,128]{2,1,0:T(8,128)(2,1)S(1)} %constant_dynamic-update-slice_fusion.refs_0_) | copy-start | bytes 786436
  11.7 13.2 %collective-permute-start.2 = (bf16[128,8,128]{2,1,0:T(8,128)(2,1)S(1)}, bf16[128,8,128]{2,1,0:T(8,128)(2,1)S(1)}, u32[]{:S(2)}, u32[]{:S(2)}) collective-permute-start(bf16[128,8,128]{2,1,0:T(8,128)(2,1)S(1)} %constant_dynamic-update-slice_fusion.refs_0_), channel_id=1, source_target_pairs={{0,1},{1,0},{2,3},{3,2},{4,5},{5,4},{6,7},{7,6},{8,9},{9,8},{10,11... | collective-permute-start | bytes 786440 | tf_op jit(solution)/shard_map/ppermute | solution.py:18
  11.8 14.9 %collective-permute-start.1 = (bf16[128,8,128]{2,1,0:T(8,128)(2,1)S(1)}, bf16[128,8,128]{2,1,0:T(8,128)(2,1)S(1)}, u32[]{:S(2)}, u32[]{:S(2)}) collective-permute-start(bf16[128,8,128]{2,1,0:T(8,128)(2,1)S(1)} %constant_dynamic-update-slice_fusion.refs_0_), channel_id=1, source_target_pairs={{0,4},{1,3},{2,6},{3,1},{4,0},{5,7},{6,2},{7,5},{8,12},{9,11},{10,... | collective-permute-start | bytes 786440 | tf_op jit(solution)/shard_map/ppermute | solution.py:18
  13.3 5.9 %collective-permute-start.14 = (bf16[64,8,128]{2,1,0:T(8,128)(2,1)S(1)}, bf16[64,8,128]{2,1,0:T(8,128)(2,1)S(1)}, u32[]{:S(2)}, u32[]{:S(2)}) collective-permute-start(bf16[64,8,128]{2,1,0:T(8,128)(2,1)S(1)} %collective-permute-done.9), channel_id=1, source_target_pairs={{0,8},{1,9},{2,10},{3,11},{4,12},{5,13},{6,14},{7,15},{8,0},{9,1},... | collective-permute-start | bytes 393224 | tf_op jit(solution)/shard_map/ppermute | solution.py:18
  13.8 5.3 %collective-permute-start.10 = (bf16[64,8,128]{2,1,0:T(8,128)(2,1)S(1)}, bf16[64,8,128]{2,1,0:T(8,128)(2,1)S(1)}, u32[]{:S(2)}, u32[]{:S(2)}) collective-permute-start(bf16[64,8,128]{2,1,0:T(8,128)(2,1)S(1)} %collective-permute-done.9), channel_id=1, source_target_pairs={{0,2},{1,5},{2,0},{3,7},{4,6},{5,1},{6,4},{7,3},{8,10},{9,13},{10,... | collective-permute-start | bytes 393224 | tf_op jit(solution)/shard_map/ppermute | solution.py:18
  15.3 5.5 %collective-permute-start.5 = (bf16[64,8,128]{2,1,0:T(8,128)(2,1)S(1)}, bf16[64,8,128]{2,1,0:T(8,128)(2,1)S(1)}, u32[]{:S(2)}, u32[]{:S(2)}) collective-permute-start(bf16[64,8,128]{2,1,0:T(8,128)(2,1)S(1)} %collective-permute-done.4), channel_id=1, source_target_pairs={{0,2},{1,5},{2,0},{3,7},{4,6},{5,1},{6,4},{7,3},{8,10},{9,13},{10,... | collective-permute-start | bytes 393224 | tf_op jit(solution)/shard_map/ppermute | solution.py:18
  19.1 3.3 %copy-start.3 = (bf16[128,8,128]{2,1,0:T(8,128)(2,1)}, bf16[128,8,128]{2,1,0:T(8,128)(2,1)S(1)}, u32[]{:S(2)}) copy-start(bf16[128,8,128]{2,1,0:T(8,128)(2,1)S(1)} %constant_dynamic-update-slice_fusion.4.refs_8_) | copy-start | bytes 786436
  19.1 9.4 %collective-permute-start.12 = (bf16[128,8,128]{2,1,0:T(8,128)(2,1)S(1)}, bf16[128,8,128]{2,1,0:T(8,128)(2,1)S(1)}, u32[]{:S(2)}, u32[]{:S(2)}) collective-permute-start(bf16[128,8,128]{2,1,0:T(8,128)(2,1)S(1)} %constant_dynamic-update-slice_fusion.4.refs_8_), channel_id=1, source_target_pairs={{0,1},{1,0},{2,3},{3,2},{4,5},{5,4},{6,7},{7,6},{8,9},{9,8},{10,11... | collective-permute-start | bytes 786440 | tf_op jit(solution)/shard_map/ppermute | solution.py:18
  19.3 5.6 %collective-permute-start.15 = (bf16[64,8,128]{2,1,0:T(8,128)(2,1)S(1)}, bf16[64,8,128]{2,1,0:T(8,128)(2,1)S(1)}, u32[]{:S(2)}, u32[]{:S(2)}) collective-permute-start(bf16[64,8,128]{2,1,0:T(8,128)(2,1)S(1)} %collective-permute-done.14), channel_id=1, source_target_pairs={{0,2},{1,5},{2,0},{3,7},{4,6},{5,1},{6,4},{7,3},{8,10},{9,13},{10,... | collective-permute-start | bytes 393224 | tf_op jit(solution)/shard_map/ppermute | solution.py:18
  20.8 7.9 %collective-permute-start.11 = (bf16[128,8,128]{2,1,0:T(8,128)(2,1)S(1)}, bf16[128,8,128]{2,1,0:T(8,128)(2,1)S(1)}, u32[]{:S(2)}, u32[]{:S(2)}) collective-permute-start(bf16[128,8,128]{2,1,0:T(8,128)(2,1)S(1)} %constant_dynamic-update-slice_fusion.4.refs_8_), channel_id=1, source_target_pairs={{0,4},{1,3},{2,6},{3,1},{4,0},{5,7},{6,2},{7,5},{8,12},{9,11},{10,... | collective-permute-start | bytes 786440 | tf_op jit(solution)/shard_map/ppermute | solution.py:18
  22.4 6.2 %copy-start = (bf16[128,8,128]{2,1,0:T(8,128)(2,1)}, bf16[128,8,128]{2,1,0:T(8,128)(2,1)S(1)}, u32[]{:S(2)}) copy-start(bf16[128,8,128]{2,1,0:T(8,128)(2,1)S(1)} %constant_dynamic-update-slice_fusion.2.refs_4_) | copy-start | bytes 786436
  24.9 4.4 %collective-permute-start.7 = (bf16[128,8,128]{2,1,0:T(8,128)(2,1)S(1)}, bf16[128,8,128]{2,1,0:T(8,128)(2,1)S(1)}, u32[]{:S(2)}, u32[]{:S(2)}) collective-permute-start(bf16[128,8,128]{2,1,0:T(8,128)(2,1)S(1)} %constant_dynamic-update-slice_fusion.2.refs_4_), channel_id=1, source_target_pairs={{0,1},{1,0},{2,3},{3,2},{4,5},{5,4},{6,7},{7,6},{8,9},{9,8},{10,11... | collective-permute-start | bytes 786440 | tf_op jit(solution)/shard_map/ppermute | solution.py:18
  24.9 3.7 %copy-start.1 = (bf16[128,8,128]{2,1,0:T(8,128)(2,1)}, bf16[128,8,128]{2,1,0:T(8,128)(2,1)S(1)}, u32[]{:S(2)}) copy-start(bf16[128,8,128]{2,1,0:T(8,128)(2,1)S(1)} %constant_dynamic-update-slice_fusion.6.refs_12_) | copy-start | bytes 786436
  24.9 3.6 %copy-start.4 = (bf16[128,8,128]{2,1,0:T(8,128)(2,1)}, bf16[128,8,128]{2,1,0:T(8,128)(2,1)S(1)}, u32[]{:S(2)}) copy-start(bf16[128,8,128]{2,1,0:T(8,128)(2,1)S(1)} %collective-permute-done.2.refs_2_) | copy-start | bytes 786436
  24.9 6.4 %collective-permute-start.6 = (bf16[128,8,128]{2,1,0:T(8,128)(2,1)S(1)}, bf16[128,8,128]{2,1,0:T(8,128)(2,1)S(1)}, u32[]{:S(2)}, u32[]{:S(2)}) collective-permute-start(bf16[128,8,128]{2,1,0:T(8,128)(2,1)S(1)} %constant_dynamic-update-slice_fusion.2.refs_4_), channel_id=1, source_target_pairs={{0,4},{1,3},{2,6},{3,1},{4,0},{5,7},{6,2},{7,5},{8,12},{9,11},{10,... | collective-permute-start | bytes 786440 | tf_op jit(solution)/shard_map/ppermute | solution.py:18
  26.7 2.0 %copy-start.5 = (bf16[128,8,128]{2,1,0:T(8,128)(2,1)}, bf16[128,8,128]{2,1,0:T(8,128)(2,1)S(1)}, u32[]{:S(2)}) copy-start(bf16[128,8,128]{2,1,0:T(8,128)(2,1)S(1)} %collective-permute-done.1.refs_1_) | copy-start | bytes 786436
  26.7 7.5 %collective-permute-start.16 = (bf16[128,8,128]{2,1,0:T(8,128)(2,1)S(1)}, bf16[128,8,128]{2,1,0:T(8,128)(2,1)S(1)}, u32[]{:S(2)}, u32[]{:S(2)}) collective-permute-start(bf16[128,8,128]{2,1,0:T(8,128)(2,1)S(1)} %constant_dynamic-update-slice_fusion.6.refs_12_), channel_id=1, source_target_pairs={{0,4},{1,3},{2,6},{3,1},{4,0},{5,7},{6,2},{7,5},{8,12},{9,11},{10,... | collective-permute-start | bytes 786440 | tf_op jit(solution)/shard_map/ppermute | solution.py:18
  28.6 7.1 %copy-start.6 = (bf16[128,8,128]{2,1,0:T(8,128)(2,1)}, bf16[128,8,128]{2,1,0:T(8,128)(2,1)S(1)}, u32[]{:S(2)}) copy-start(bf16[128,8,128]{2,1,0:T(8,128)(2,1)S(1)} %collective-permute-done.12.refs_10_) | copy-start | bytes 786436
  28.6 6.3 %collective-permute-start.17 = (bf16[128,8,128]{2,1,0:T(8,128)(2,1)S(1)}, bf16[128,8,128]{2,1,0:T(8,128)(2,1)S(1)}, u32[]{:S(2)}, u32[]{:S(2)}) collective-permute-start(bf16[128,8,128]{2,1,0:T(8,128)(2,1)S(1)} %constant_dynamic-update-slice_fusion.6.refs_12_), channel_id=1, source_target_pairs={{0,1},{1,0},{2,3},{3,2},{4,5},{5,4},{6,7},{7,6},{8,9},{9,8},{10,11... | collective-permute-start | bytes 786440 | tf_op jit(solution)/shard_map/ppermute | solution.py:18
  28.7 7.0 %copy-start.7 = (bf16[128,8,128]{2,1,0:T(8,128)(2,1)}, bf16[128,8,128]{2,1,0:T(8,128)(2,1)S(1)}, u32[]{:S(2)}) copy-start(bf16[128,8,128]{2,1,0:T(8,128)(2,1)S(1)} %collective-permute-done.11.refs_9_) | copy-start | bytes 786436
  28.7 6.2 %collective-permute-start.3 = (bf16[128,8,128]{2,1,0:T(8,128)(2,1)S(1)}, bf16[128,8,128]{2,1,0:T(8,128)(2,1)S(1)}, u32[]{:S(2)}, u32[]{:S(2)}) collective-permute-start(bf16[128,8,128]{2,1,0:T(8,128)(2,1)S(1)} %collective-permute-done.1.refs_1_), channel_id=1, source_target_pairs={{0,1},{1,0},{2,3},{3,2},{4,5},{5,4},{6,7},{7,6},{8,9},{9,8},{10,11... | collective-permute-start | bytes 786440 | tf_op jit(solution)/shard_map/ppermute | solution.py:18
  29.2 6.5 %copy-start.8 = (bf16[128,8,128]{2,1,0:T(8,128)(2,1)}, bf16[128,8,128]{2,1,0:T(8,128)(2,1)S(1)}, u32[]{:S(2)}) copy-start(bf16[128,8,128]{2,1,0:T(8,128)(2,1)S(1)} %collective-permute-done.7.refs_6_) | copy-start | bytes 786436
  29.2 5.6 %collective-permute-start.13 = (bf16[128,8,128]{2,1,0:T(8,128)(2,1)S(1)}, bf16[128,8,128]{2,1,0:T(8,128)(2,1)S(1)}, u32[]{:S(2)}, u32[]{:S(2)}) collective-permute-start(bf16[128,8,128]{2,1,0:T(8,128)(2,1)S(1)} %collective-permute-done.11.refs_9_), channel_id=1, source_target_pairs={{0,1},{1,0},{2,3},{3,2},{4,5},{5,4},{6,7},{7,6},{8,9},{9,8},{10,11... | collective-permute-start | bytes 786440 | tf_op jit(solution)/shard_map/ppermute | solution.py:18
  31.4 4.4 %copy-start.9 = (bf16[128,8,128]{2,1,0:T(8,128)(2,1)}, bf16[128,8,128]{2,1,0:T(8,128)(2,1)S(1)}, u32[]{:S(2)}) copy-start(bf16[128,8,128]{2,1,0:T(8,128)(2,1)S(1)} %collective-permute-done.6.refs_5_) | copy-start | bytes 786436
  31.4 3.5 %collective-permute-start.8 = (bf16[128,8,128]{2,1,0:T(8,128)(2,1)S(1)}, bf16[128,8,128]{2,1,0:T(8,128)(2,1)S(1)}, u32[]{:S(2)}, u32[]{:S(2)}) collective-permute-start(bf16[128,8,128]{2,1,0:T(8,128)(2,1)S(1)} %collective-permute-done.6.refs_5_), channel_id=1, source_target_pairs={{0,1},{1,0},{2,3},{3,2},{4,5},{5,4},{6,7},{7,6},{8,9},{9,8},{10,11... | collective-permute-start | bytes 786440 | tf_op jit(solution)/shard_map/ppermute | solution.py:18
  34.2 1.5 %collective-permute-start.18 = (bf16[128,8,128]{2,1,0:T(8,128)(2,1)S(1)}, bf16[128,8,128]{2,1,0:T(8,128)(2,1)S(1)}, u32[]{:S(2)}, u32[]{:S(2)}) collective-permute-start(bf16[128,8,128]{2,1,0:T(8,128)(2,1)S(1)} %collective-permute-done.16.refs_13_), channel_id=1, source_target_pairs={{0,1},{1,0},{2,3},{3,2},{4,5},{5,4},{6,7},{7,6},{8,9},{9,8},{10,11... | collective-permute-start | bytes 786440 | tf_op jit(solution)/shard_map/ppermute | solution.py:18
  (6 other events, 5.9 us)
